TPU v7x, 32 devices: a whole 2x2x4 slice. The times are simulated.
32 devices in a mesh: island: 2 (over core), dp: 4 (over z), tensor: 4 (over y, x).
Axes of the slice: x: 2, y: 2, z: 4, core: 2. Of those that a mesh axis runs over, the one named last changes fastest.
Arguments:
- pseudo_grad: float32 [2, 48, 256, 5120], P('island', None, 'dp', 'tensor'), may hold values from -1000 to 1000, as said below
- block_owner: int32 [48], replicated, may hold values from 0 to 7, as said below
Outputs:
- update: bfloat16 [8, 12, 256, 5120], P(('island', 'dp'), None, None, 'tensor')
Inputs may be any that keep to these rules, and one draw needn't show every extreme that they name: `pseudo_grad`: float pseudo-gradients; entries lie within the range. `block_owner`: every owner holds at most 12 blocks and at least one; some owner holds exactly 12.
All inputs are finite; a program needn't handle non-finite values.
Results may differ from a plain program's by a relative error of at most 0.001.
Values sent between devices are 32-bit elements; how exact they have to be, the bound alone decides.
A program may use at most 128 MiB of HBM per device.

v0:
```python
import math
import jax
import jax.numpy as jnp
from jax import lax
from jax.sharding import PartitionSpec as P

D = 5120
COEF_A = 3.4445
COEF_B = -4.775
COEF_C = 2.0315
EPSILON = 1e-07


def slot_table(block_owner, owner_count, slot_count):
    blocks = block_owner.shape[0]
    positions = jnp.arange(blocks, dtype=jnp.int32)
    one_hot = (block_owner[:, None] == jnp.arange(owner_count, dtype=jnp.int32)[None, :]).astype(
        jnp.float32
    )
    earlier = (positions[None, :] < positions[:, None]).astype(jnp.float32)
    counts_before = jnp.dot(earlier, one_hot, precision=lax.Precision.HIGHEST)
    slot = jnp.sum(counts_before * one_hot, axis=1).astype(jnp.int32)
    slot_key = block_owner * slot_count + slot
    entries = jnp.arange(owner_count * slot_count, dtype=jnp.int32)
    matches = slot_key[None, :] == entries[:, None]
    slot_index = jnp.sum(jnp.where(matches, positions[None, :], 0), axis=1)
    slot_valid = jnp.any(matches, axis=1)
    return (slot_index, slot_valid)


def batch_dot(left, right):
    return jnp.einsum("khg,kgc->khc", left, right, precision=lax.Precision.HIGHEST)


def polynomial(gram_mat):
    return COEF_B * gram_mat + COEF_C * batch_dot(gram_mat, gram_mat)


def orthogonalize(incoming):
    blocks = incoming[0]
    partial_value = jnp.einsum("khc,kgc->khg", blocks, blocks, precision=lax.Precision.HIGHEST)
    gram_first = lax.psum(partial_value, "tensor")
    squares = jnp.trace(gram_first, axis1=1, axis2=2)
    inverse = 1.0 / (jnp.sqrt(squares) + EPSILON)
    start = blocks * inverse[:, None, None]
    gram_start = gram_first * (inverse * inverse)[:, None, None]
    poly_first = polynomial(gram_start)
    identity = jnp.eye(blocks.shape[1], dtype=jnp.float32)[None]
    first_factor = COEF_A * identity + poly_first
    gram_second = batch_dot(batch_dot(first_factor, gram_start), first_factor)
    second_factor = COEF_A * identity + polynomial(gram_second)
    final = batch_dot(batch_dot(second_factor, first_factor), start)
    return (math.sqrt(D) * final).astype(jnp.bfloat16)[None]


def body(pseudo_grad, block_owner):
    own_grad = pseudo_grad[0]
    blocks = block_owner.shape[0]
    dp_count = lax.axis_size("dp")
    island_count = lax.axis_size("island")
    owner_count = island_count * dp_count
    slot_count = 2 * (blocks // owner_count)
    row_count = own_grad.shape[1]
    col_count = own_grad.shape[2]
    slot_index, slot_valid = slot_table(block_owner, owner_count, slot_count)
    summed = lax.psum(own_grad, "island")
    island = lax.axis_index("island")
    own_index = lax.dynamic_slice_in_dim(
        slot_index, island * dp_count * slot_count, dp_count * slot_count
    )
    own_valid = lax.dynamic_slice_in_dim(
        slot_valid, island * dp_count * slot_count, dp_count * slot_count
    )
    picked = jnp.take(summed, own_index, axis=0)
    picked = jnp.where(own_valid[:, None, None], picked, 0.0)
    outgoing = picked.reshape(dp_count, slot_count, row_count, col_count)
    return orthogonalize(lax.all_to_all(outgoing, "dp", split_axis=0, concat_axis=2, tiled=True))


def solution(mesh):
    in_specs = (P("island", None, "dp", "tensor"), P())
    out_specs = P(("island", "dp"), None, None, "tensor")
    return jax.shard_map(body, mesh=mesh, in_specs=in_specs, out_specs=out_specs, check_vma=False)
```

profile of v0, /device:TPU:0, one launch (start us, length us, event | category | flops | bytes accessed | tf_op | source)
XLA Modules:
  0.0 606.4 jit_solution(15884312456623883124)
XLA Ops:
  6.5 0.0 all-reduce.3.cloned.1.call-start
  6.5 0.0 copy-start.1
  6.5 0.7 all-reduce.3.cloned.1.call-update
  7.3 0.0 all-reduce.5.cloned.1.call-start
  7.3 0.0 copy-done.1
  7.3 0.1 fusion.36
  7.5 0.1 select_reduce_fusion.1
  7.6 0.1 compare_and_fusion
  7.7 0.1 broadcast_in_dim.67
  7.7 0.1 fusion.37
  7.8 0.1 dynamic_slice.6
  7.9 0.1 broadcast_in_dim.63
  8.0 60.4 %all-reduce.3.cloned.1.call-done = f32[48,64,1280]{2,1,0:T(8,128)} async-done(((f32[48,64,1280]{2,1,0:T(8,128)}), f32[48,64,1280]{2,1,0:T(8,128)}) %all-reduce.3.cloned.1.call-update) | async-done | bytes 15728656 | tf_op jit(solution)/shard_map/psum | solution.py:66
  68.4 14.6 %gather_fusion = f32[48,64,1280]{2,1,0:T(8,128)} fusion(f32[48,64,1280]{2,1,0:T(8,128)} %all-reduce.3.cloned.1.call-done, s32[1024]{0:T(1024)S(1)} %pad_clamp_fusion), kind=kCustom, calls=%fused_computation | custom fusion | bytes 31457472 | tf_op jit(solution)/shard_map/jit(_take)/gather | solution.py:74
  83.0 6.7 %select_select_fusion = f32[4,12,64,1280]{3,2,1,0:T(8,128)S(1)} fusion(f32[4,12,64,1280]{3,2,1,0:T(8,128)} %bitcast.16, pred[4,12]{1,0:T(4,128)(4,1)S(1)} %broadcast_in_dim.67, pred[4,12]{1,0:T(4,128)(4,1)S(1)} %broadcast_in_dim.63), kind=kLoop, calls=%fused_computation.4 | loop fusion | flops 7864320 | bytes 31457376 | tf_op jit(solution)/shard_map/jit(_where)/select_n | solution.py:75
  89.6 345.5 %all_to_all.15 = f32[4,12,64,1280]{3,2,1,0:T(8,128)} all-to-all(f32[4,12,64,1280]{3,2,1,0:T(8,128)S(1)} %select_select_fusion), channel_id=1, replica_groups=mesh['island'=2,'dp'=4,'tensor'=4] {'dp'}, dimensions={0} | all-to-all | bytes 31457280 | tf_op jit(solution)/shard_map/all_to_all | solution.py:77
  435.1 12.7 %copy.7 = f32[1,12,4,64,1280]{4,3,2,1,0:T(8,128)} copy(f32[1,12,4,64,1280]{4,3,1,2,0:T(8,128)} %bitcast.17) | data formatting | bytes 31457280 | tf_op jit(solution)/shard_map/all_to_all | solution.py:77
  447.9 21.9 %fusion.46 = f32[12,256,256]{2,1,0:T(8,128)} fusion(f32[12,256,1280]{2,1,0:T(8,128)} %bitcast.14), kind=kOutput, calls=%fused_computation.59 | convolution fusion | flops 12079595520 | bytes 18874368 | tf_op jit(solution)/shard_map/khc,kgc->khg/dot_general | solution.py:41
  469.8 0.0 all-reduce.5.cloned.1.call-update
  469.9 86.2 %all-reduce.5.cloned.1.call-done = f32[12,256,256]{2,1,0:T(8,128)} async-done(((f32[12,256,256]{2,1,0:T(8,128)}), f32[12,256,256]{2,1,0:T(8,128)}) %all-reduce.5.cloned.1.call-update) | async-done | bytes 3145744 | tf_op jit(solution)/shard_map/psum | solution.py:42
  556.1 0.0 copy-start
  556.1 2.5 select_reduce_fusion
  558.6 0.3 copy-done
  558.9 3.4 fusion.20
  562.4 4.1 fusion.14
  566.5 3.8 fusion.13
  570.4 3.7 fusion.47
  574.1 4.5 fusion.8
  578.6 20.8 %fusion.5 = bf16[1,12,256,1280]{3,2,1,0:T(8,128)(2,1)} fusion(f32[12,256,256]{2,1,0:T(8,128)S(1)} %fusion.8, f32[12,256,1280]{2,1,0:T(8,128)} %bitcast.15, f32[12]{0:T(128)S(1)} %get-tuple-element.6), kind=kOutput, calls=%fused_computation.6 | convolution fusion | flops 12091392000 | bytes 26738736 | tf_op jit(solution)/shard_map/khg,kgc->khc/dot_general | solution.py:32
  (5 shorter events, 0.1 us)
Async XLA Ops:
  6.5 61.9 %all-reduce.3.cloned.1.call-start = ((), (), s32[]{:S(2)}) async-start(), calls=%async_computation.1 | async-start | bytes 31457280 | tf_op jit(solution)/shard_map/psum | solution.py:66
  6.5 0.8 copy-start.1
  7.3 548.8 %all-reduce.5.cloned.1.call-start = ((), (), s32[]{:S(2)}) async-start(), calls=%async_computation.2 | async-start | bytes 6291456 | tf_op jit(solution)/shard_map/psum | solution.py:42
  556.1 2.8 copy-start
Sparse Core Ops, SparseCore 0:
  9.8 58.5 all-reduce.2
  470.0 86.0 all-reduce.4
where the time goes:
time: 613 us; the launch traced here: 606 us
  blocking collectives  346 us (56%)
  waiting for transfers between devices  147 us (24%)
  matrix products  62.5 us (10%)
  local copies, waits for them, and re-layouts  27.9 us (5%)
  between operations  13.7 us (2%)
  other arithmetic  9.49 us (2%)
    all_to_all x1, blocking collectives, body(): lax.all_to_all(outgoing, 'dp', split_axis=0, concat_axis=2, tiled=True)  346 us
    psum x1, waiting for transfers between devices, orthogonalize(): gram_first = lax.psum(partial_value, 'tensor')  86.2 us
    psum x1, waiting for transfers between devices, body(): summed = lax.psum(own_grad, 'island')  60.4 us
    dot_general x6, matrix products, batch_dot(): jnp.einsum('khg,kgc->khc', left, right, precision=lax.Precision.HIGHEST)  40.4 us
    dot_general x1, matrix products, orthogonalize(): jnp.einsum('khc,kgc->khg', blocks, blocks, precision=lax.Precision.HIGHEST)  21.9 us
    gather x1, local copies, waits for them, and re-layouts, body(): picked = jnp.take(summed, own_index, axis=0)  14.6 us
    all_to_all x1, local copies, waits for them, and re-layouts, body(): lax.all_to_all(outgoing, 'dp', split_axis=0, concat_axis=2, tiled=True)  12.7 us
  transfers between devices with their start and end apart: 2, of which 2 were waited for; matrix products, arithmetic and copies ran while one was open for 0% of the time, Pallas kernels for 0%

commit v1 on v0

--- a/solution.py
+++ b/solution.py
@@ -9,6 +9,14 @@
 COEF_B = -4.775
 COEF_C = 2.0315
 EPSILON = 1e-07
+
+
+def _recover_row(local):
+    current_arr = jax.lax.axis_size("dp")
+    f_next = jnp.split(local, current_arr, axis=0)
+    frame_out = jnp.stack(f_next)
+    response = jax.lax.all_to_all(frame_out, axis_name="dp", split_axis=0, concat_axis=0)
+    return jnp.concatenate(response, axis=2)
 
 
 def slot_table(block_owner, owner_count, slot_count):
@@ -74,7 +82,7 @@
     picked = jnp.take(summed, own_index, axis=0)
     picked = jnp.where(own_valid[:, None, None], picked, 0.0)
     outgoing = picked.reshape(dp_count, slot_count, row_count, col_count)
-    return orthogonalize(lax.all_to_all(outgoing, "dp", split_axis=0, concat_axis=2, tiled=True))
+    return orthogonalize(_recover_row(outgoing))
 
 
 def solution(mesh):

time: 613 us -> 636 us (1.038)
  local copies, waits for them, and re-layouts: 27.9 us -> 39.3 us
  other arithmetic: 9.49 us -> 20.6 us
    reshape x0 -> x1, local copies, waits for them, and re-layouts: none -> 12.7 us  [_recover_row(): return jnp.concatenate(response, axis=2)]
    all_to_all x1 -> x0, local copies, waits for them, and re-layouts: 12.7 us -> none  [body(): lax.all_to_all(outgoing, 'dp', split_axis=0, concat_axis=2, tiled=True)]
    another operation x0 -> x1, local copies, waits for them, and re-layouts: none -> 11.6 us  [_recover_row(): frame_out = jnp.stack(f_next)]
where the time goes in v1:
time: 636 us; the launch traced here: 629 us
  blocking collectives  346 us (54%)
  waiting for transfers between devices  147 us (23%)
  matrix products  62.4 us (10%)
  local copies, waits for them, and re-layouts  39.3 us (6%)
  other arithmetic  20.6 us (3%)
  between operations  13.7 us (2%)
    all_to_all x1, blocking collectives, _recover_row(): jax.lax.all_to_all(frame_out, axis_name='dp', split_axis=0, concat_axis=0)  346 us
    psum x1, waiting for transfers between devices, orthogonalize(): gram_first = lax.psum(partial_value, 'tensor')  86.2 us
    psum x1, waiting for transfers between devices, body(): summed = lax.psum(own_grad, 'island')  60.6 us
    dot_general x6, matrix products, batch_dot(): jnp.einsum('khg,kgc->khc', left, right, precision=lax.Precision.HIGHEST)  40.1 us
    dot_general x1, matrix products, orthogonalize(): jnp.einsum('khc,kgc->khg', blocks, blocks, precision=lax.Precision.HIGHEST)  22.1 us
    gather x1, local copies, waits for them, and re-layouts, body(): picked = jnp.take(summed, own_index, axis=0)  14.6 us
    reshape x1, local copies, waits for them, and re-layouts, _recover_row(): return jnp.concatenate(response, axis=2)  12.7 us
  transfers between devices with their start and end apart: 2, of which 2 were waited for; matrix products, arithmetic and copies ran while one was open for 0% of the time, Pallas kernels for 0%

profile of v1, /device:TPU:0, one launch (start us, length us, event | category | flops | bytes accessed | tf_op | source)
XLA Modules:
  0.0 629.1 jit_solution(16390810250004174804)
XLA Ops:
  6.5 0.0 all-reduce.3.cloned.1.call-start
  6.5 0.0 copy-start.1
  6.5 0.7 all-reduce.3.cloned.1.call-update
  7.3 0.0 all-reduce.5.cloned.1.call-start
  7.3 0.0 copy-done.1
  7.3 0.1 fusion.36
  7.5 0.1 fusion.37
  7.6 0.1 dynamic_slice.6
  7.6 0.1 select_reduce_fusion.1
  7.7 0.1 compare_and_fusion
  7.8 60.6 %all-reduce.3.cloned.1.call-done = f32[48,64,1280]{2,1,0:T(8,128)} async-done(((f32[48,64,1280]{2,1,0:T(8,128)}), f32[48,64,1280]{2,1,0:T(8,128)}) %all-reduce.3.cloned.1.call-update) | async-done | bytes 15728656 | tf_op jit(solution)/shard_map/psum | solution.py:74
  68.4 14.6 %gather_fusion = f32[48,64,1280]{2,1,0:T(8,128)} fusion(f32[48,64,1280]{2,1,0:T(8,128)} %all-reduce.3.cloned.1.call-done, s32[1024]{0:T(1024)S(1)} %pad_clamp_fusion), kind=kCustom, calls=%fused_computation | custom fusion | bytes 31457472 | tf_op jit(solution)/shard_map/jit(_take)/gather | solution.py:82
  83.0 11.5 %select_select_fusion = f32[48,64,1280]{2,1,0:T(8,128)} fusion(f32[48,64,1280]{2,1,0:T(8,128)} %gather_fusion, pred[48]{0:T(512)(128)(4,1)S(1)} %get-tuple-element.7, pred[48]{0:T(512)(128)(4,1)S(1)} %dynamic_slice.6), kind=kLoop, calls=%fused_computation.5 | loop fusion | flops 7864320 | bytes 31457376 | tf_op jit(solution)/shard_map/jit(_where)/select_n | solution.py:83
  94.5 11.6 %slice_bitcast_fusion.3 = (f32[1,1,12,64,1280]{4,3,2,1,0:T(8,128)}, f32[1,1,12,64,1280]{4,3,2,1,0:T(8,128)}, f32[1,1,12,64,1280]{4,3,2,1,0:T(8,128)}, f32[1,1,12,64,1280]{4,3,2,1,0:T(8,128)}) fusion(f32[48,64,1280]{2,1,0:T(8,128)} %select_select_fusion), kind=kLoop, calls=%fused_computation.11 | loop fusion | bytes 31457280 | tf_op jit(solution)/shard_map/stack | solution.py:17
  106.1 6.3 pad_maximum_fusion
  112.3 345.5 %all_to_all.5 = f32[4,1,12,64,1280]{4,3,2,1,0:T(8,128)} all-to-all(f32[4,1,12,64,1280]{4,3,2,1,0:T(8,128)S(1)} %pad_maximum_fusion), channel_id=1, replica_groups=mesh['island'=2,'dp'=4,'tensor'=4] {'dp'}, dimensions={0} | all-to-all | bytes 31457280 | tf_op jit(solution)/shard_map/all_to_all | solution.py:18
  457.8 12.7 %copy.4 = f32[1,12,4,64,1280]{4,3,2,1,0:T(8,128)} copy(f32[1,12,4,64,1280]{4,3,1,0,2:T(8,128)} %bitcast.21) | data formatting | bytes 31457280 | tf_op jit(solution)/shard_map/reshape | solution.py:19
  470.6 22.1 %fusion.46 = f32[12,256,256]{2,1,0:T(8,128)} fusion(f32[12,256,1280]{2,1,0:T(8,128)} %bitcast.19), kind=kOutput, calls=%fused_computation.64 | convolution fusion | flops 12079595520 | bytes 18874368 | tf_op jit(solution)/shard_map/khc,kgc->khg/dot_general | solution.py:49
  492.7 0.0 all-reduce.5.cloned.1.call-update
  492.8 86.2 %all-reduce.5.cloned.1.call-done = f32[12,256,256]{2,1,0:T(8,128)} async-done(((f32[12,256,256]{2,1,0:T(8,128)}), f32[12,256,256]{2,1,0:T(8,128)}) %all-reduce.5.cloned.1.call-update) | async-done | bytes 3145744 | tf_op jit(solution)/shard_map/psum | solution.py:50
  579.0 0.0 copy-start
  579.0 2.5 select_reduce_fusion
  581.5 0.3 copy-done
  581.8 3.4 fusion.20
  585.3 4.1 fusion.14
  589.4 3.8 fusion.13
  593.2 3.4 fusion.47
  596.7 4.5 fusion.8
  601.2 20.8 %fusion.5 = bf16[1,12,256,1280]{3,2,1,0:T(8,128)(2,1)} fusion(f32[12,256,256]{2,1,0:T(8,128)S(1)} %fusion.8, f32[12,256,1280]{2,1,0:T(8,128)} %bitcast.20, f32[12]{0:T(128)S(1)} %get-tuple-element.6), kind=kOutput, calls=%fused_computation.7 | convolution fusion | flops 12091392000 | bytes 26738736 | tf_op jit(solution)/shard_map/khg,kgc->khc/dot_general | solution.py:40
  (5 shorter events, 0.1 us)
Async XLA Ops:
  6.5 61.9 %all-reduce.3.cloned.1.call-start = ((), (), s32[]{:S(2)}) async-start(), calls=%async_computation.1 | async-start | bytes 31457280 | tf_op jit(solution)/shard_map/psum | solution.py:74
  6.5 0.8 copy-start.1
  7.3 571.7 %all-reduce.5.cloned.1.call-start = ((), (), s32[]{:S(2)}) async-start(), calls=%async_computation.2 | async-start | bytes 6291456 | tf_op jit(solution)/shard_map/psum | solution.py:50
  579.0 2.8 copy-start
Sparse Core Ops, SparseCore 0:
  9.8 58.5 all-reduce.2
  492.9 86.0 all-reduce.4
